TPU v7x, 256 devices: a whole 4x4x8 slice. The times are simulated.
256 devices in a mesh: tm: 64 (over z_lo, y, x), space: 4 (over z_hi, core).
Axes of the slice: x: 4, y: 4, z: 8 (z_hi: 2, z_lo: 4; z = z_hi * 4 + z_lo), core: 2. Of those that a mesh axis runs over, the one named last changes fastest.
Arguments:
- state_field: float32 [128, 16, 16, 128], P('tm', 'space'), may hold values from -3 to 3
- adjoint: float32 [128, 16, 16, 128], P('tm', 'space'), may hold values from -3 to 3
- target: float32 [128, 16, 16, 128], P('tm', 'space'), may hold values from -4 to 4
- initial_state: float32 [16, 16, 128], P('space'), may hold values from -4 to 4
- conductivity: float32 [16, 16, 128], P('space'), may hold values from 0.05 to 0.5
- reaction: float32 [16, 16, 128], P('space'), may hold values from 0.05 to 1
Outputs:
- new_state: float32 [128, 16, 16, 128], P('tm', 'space')
- new_adjoint: float32 [128, 16, 16, 128], P('tm', 'space')
All inputs are finite; a program needn't handle non-finite values.
Results may differ from a plain program's by a relative error of at most 0.00029.
Values sent between devices are 32-bit elements; how exact they have to be, the bound alone decides.
No kernel may reach another device: no remote copies, remote signals or barrier semaphores. Data moves between devices by JAX's collectives and lax.ppermute only.
A program may use at most 64 MiB of HBM per device.

v0:
```python
import functools

import jax
import jax.numpy as jnp
import numpy as np
from jax import lax
from jax.experimental import pallas as pl
from jax.experimental.pallas import tpu as pltpu
from jax.sharding import PartitionSpec as P


CHEB = 8
step_rate = 2.0
coupling = 1.0
lower_edge = 0.05
upper_edge = 7.0
COEF = 16
vmem = functools.partial(pl.BlockSpec, memory_space=pltpu.VMEM)
grant = pltpu.CompilerParams(vmem_limit_bytes=8 * 1024 * 1024)
hbm = functools.partial(pl.BlockSpec, memory_space=pltpu.HBM)


def time_tables(horizon, slots):
    k = np.arange(slots)[:, None]
    n = np.concatenate([np.arange(0, horizon, 2), np.arange(1, horizon, 2)])[None, :]
    angle = 2.0 * np.pi / horizon * ((k * n) % horizon)
    cosine, sine = np.cos(angle), np.sin(angle)
    alternation = np.where(n % 2 == 0, 1.0, -1.0)
    forward = np.concatenate([cosine, np.where(k == 0, alternation, -sine)], 0)
    inverse = (
        np.concatenate(
            [
                np.where(k == 0, 1.0, 2.0) * cosine,
                np.where(k == 0, alternation, -2.0 * sine),
            ],
            0,
        )
        / horizon
    )
    return forward.astype(np.float32), inverse.T.astype(np.float32)


def solver_table(horizon, slots):
    theta = 2.0 * np.pi / horizon * np.arange(slots + 1)
    shift = step_rate * (1.0 - np.cos(theta))
    twist = step_rate * np.sin(theta)
    twist[slots] = 0.0
    spread = twist * twist + coupling
    lower = (lower_edge + shift) ** 2 + spread
    upper = (upper_edge + shift) ** 2 + spread
    centre = 0.5 * (upper + lower)
    half = 0.5 * (upper - lower)
    ratio = centre / half
    gamma = np.sqrt(2.0 / half)
    offset = np.sqrt(2.0 * (centre - spread) / half)
    table = np.zeros((slots + 1, COEF))
    table[:, 0] = gamma
    table[:, 1] = offset
    table[:, 2] = shift
    table[:, 3] = 1.0 / gamma
    table[:, 4] = offset / gamma
    nodes = np.pi * (np.arange(CHEB) + 0.5) / CHEB
    points = np.cos(nodes)[None, :]
    value = centre[:, None] + half[:, None] * points
    top = np.cosh(CHEB * np.arccosh(ratio))[:, None]
    samples = (1.0 - np.cos(CHEB * np.arccos(-points)) / top) / value
    for j in range(CHEB):
        weight = (1.0 if j == 0 else 2.0) / CHEB
        table[:, 5 + j] = weight * np.sum(samples * np.cos(j * nodes)[None, :], 1)
    rows = np.broadcast_to(table.reshape(-1, 1), (table.size, 128))
    return rows.astype(np.float32), twist[:slots]


def twist_block(twist):
    block = np.zeros((twist.shape[0], 128), np.float32)
    block[:, 0] = twist
    return block


def rows_of(count, start, stride):
    return pl.ds(start, count, stride=stride)


def pack_kernel(c_hbm, r_hbm, y_hbm, p_hbm, t_hbm, o_ref, m_ref, y_ref, p_ref, t_ref, sem):
    copies = [
        pltpu.make_async_copy(source, target, sem.at[i])
        for i, (source, target) in enumerate(
            (
                (y_hbm, y_ref),
                (p_hbm, p_ref),
                (t_hbm, t_ref),
                (c_hbm, m_ref.at[0]),
                (r_hbm, m_ref.at[1]),
            )
        )
    ]
    for copy in copies:
        copy.start()
    for copy in copies:
        copy.wait()
    rows = y_ref.shape[1]
    for i, ref in enumerate((y_ref, p_ref, t_ref)):
        for j in range(2):
            o_ref[rows_of(rows, 2 * i + j, 6), :] = ref[j]


def halves(value):
    high = value.astype(jnp.bfloat16)
    return high, (value - high.astype(jnp.float32)).astype(jnp.bfloat16)


def product(high, low, data):
    data_high, data_low = halves(data)
    dot = functools.partial(lax.dot, preferred_element_type=jnp.float32)
    return dot(high, data_high) + (dot(high, data_low) + dot(low, data_high))


def forward_kernel(fh_ref, fl_ref, init_ref, x_ref, o_ref):
    rows = x_ref.shape[0] // 6
    lanes = x_ref.shape[1]
    mine = lax.axis_index("tm")
    y0, y1, p0, p1, t0, t1 = (x_ref[rows_of(rows, i, 6), :] for i in range(6))
    g0, g1 = (y * y * y * (1.0 / 3.0) + coupling * p for y, p in ((y0, p0), (y1, p1)))
    h0, h1 = (y * y * p - y + t for y, p, t in ((y0, p0, t0), (y1, p1, t1)))
    row = lax.broadcasted_iota(jnp.int32, (rows, lanes), 0)
    before = jnp.where(row == 0, init_ref[pl.ds(mine, 1), :], pltpu.roll(y1, 1, 0))
    after = jnp.where(row == rows - 1, 0.0, pltpu.roll(p0, rows - 1, 0))
    a0 = g0 + step_rate * (y0 - before)
    a1 = g1 + step_rate * (y1 - y0)
    b0 = h0 + step_rate * (p0 - p1)
    b1 = h1 + step_rate * (p1 - after)
    data = jnp.concatenate(
        [
            jnp.concatenate([a0, b0, y0, p0], 1),
            jnp.concatenate([a1, b1, y1, p1], 1),
        ],
        0,
    )
    hat = product(fh_ref[...], fl_ref[...], data)
    for f in range(2):
        for r in range(2):
            for q in range(2):
                column = (q * 2 + f) * lanes
                o_ref[rows_of(rows, (f * 2 + r) * 2 * rows + q, 2), :] = hat[
                    r * rows : (r + 1) * rows, column : column + lanes
                ]


def coefficients(co_ref, slots, subs):
    slot = lax.axis_index("tm")
    item = lax.axis_index("space")
    base = jnp.where((slot == 0) & (item % 2 == 1), slots, slot) * COEF
    lanes = co_ref.shape[1]
    return item, lambda j: jnp.broadcast_to(co_ref[pl.ds(base + j, 1), :], (subs, lanes))


def faces_kernel(
    slots,
    co_ref,
    m0_ref,
    m1_ref,
    m2_ref,
    m3_ref,
    cx,
    cy,
    cy_next,
    cy_last,
    cz_next,
    cz_last,
    bare,
    plus,
    minus,
    mat,
):
    item, coefficient = coefficients(co_ref, slots, cx.shape[2])
    gamma, offset, shift = (coefficient(j) for j in range(3))
    for piece, ref in enumerate((m0_ref, m1_ref, m2_ref, m3_ref)):
        mat[item ^ piece] = ref[...]
    count, _, subs, lanes = cx.shape
    width = mat.shape[2]
    sub = lax.broadcasted_iota(jnp.int32, (subs, lanes), 0)
    lane = lax.broadcasted_iota(jnp.int32, (subs, lanes), 1)
    first, last = sub == 0, sub == subs - 1
    left, right = lane == 0, lane == lanes - 1

    def part(which, x, parity):
        return mat.at[x // width, which, x % width][rows_of(subs, parity, 2), :]

    for x in range(count):
        even, odd = part(0, x, 0), part(0, x, 1)
        pair = 0.5 * (even + odd)
        after = 0.5 * odd + jnp.where(last, 0.0, 0.5 * pltpu.roll(even, subs - 1, 0))
        before = 0.5 * even + jnp.where(first, 0.0, 0.5 * pltpu.roll(odd, 1, 0))
        cy[x] = gamma * pair
        cy_next[x] = gamma * jnp.where(last, 0.0, after)
        cy_last[x] = gamma * jnp.where(first, 0.0, before)
        for parity, (c, side) in enumerate(((even, before), (odd, after))):
            half = 0.5 * c
            up = half + 0.5 * part(0, x + 1, parity) if x + 1 < count else half
            down = half + 0.5 * part(0, x - 1, parity) if x > 0 else half
            zn = half + jnp.where(right, 0.0, 0.5 * pltpu.roll(c, lanes - 1, 1))
            zl = half + jnp.where(left, 0.0, 0.5 * pltpu.roll(c, 1, 1))
            cx[x, parity] = gamma * up
            cz_next[x, parity] = gamma * jnp.where(right, 0.0, zn)
            cz_last[x, parity] = gamma * jnp.where(left, 0.0, zl)
            total = (up + down) + (pair + side) + (zn + zl)
            bare[x, parity] = gamma * total
            full = gamma * (total + part(1, x, parity) + shift)
            plus[x, parity] = full + offset
            minus[x, parity] = full - offset


def solve_kernel(
    slots,
    co_ref,
    cx,
    cy,
    cy_next,
    cy_last,
    cz_next,
    cz_last,
    bare,
    plus,
    minus,
    x_ref,
    o_ref,
    res,
    b0,
    b1,
    t,
):
    count, _, subs, lanes = cx.shape
    coefficient = coefficients(co_ref, slots, subs)[1]
    cells = x_ref.shape[0] // 8
    line = 2 * subs
    width = cells // line

    def place(x, parity, field):
        start = (x // width * cells + x % width * line + parity) * 2 + field
        return rows_of(subs, start, 4)

    def sweep(load, diag, emit):
        now, cx_now = load(0), None
        last = cx_last = None
        for x in range(count):
            after = load(x + 1) if x + 1 < count else None
            cx_now = (cx[x, 0], cx[x, 1]) if x + 1 < count else None
            pair = cy[x]
            side = (
                pair * now[1] + cy_last[x] * pltpu.roll(now[1], 1, 0),
                pair * now[0] + cy_next[x] * pltpu.roll(now[0], subs - 1, 0),
            )
            for parity in range(2):
                v = now[parity]
                out = diag[x, parity] * v - side[parity]
                lateral = cz_next[x, parity] * pltpu.roll(v, lanes - 1, 1)
                lateral = lateral + cz_last[x, parity] * pltpu.roll(v, 1, 1)
                if after is not None:
                    out = out - cx_now[parity] * after[parity]
                if last is not None:
                    lateral = lateral + cx_last[parity] * last[parity]
                emit(x, parity, out - lateral, v)
            last, now, cx_last = now, after, cx_now

    def kept(ref):
        return lambda x: (ref[x, 0], ref[x, 1])

    inverse_gamma = coefficient(3)
    top = coefficient(5 + CHEB - 1)

    def begin(x, parity, out, v):
        r = x_ref[place(x, parity, 0), :] + inverse_gamma * out
        res[x, parity] = r
        b0[x, parity] = top * r
        b1[x, parity] = jnp.zeros_like(r)

    sweep(
        lambda x: (x_ref[place(x, 0, 1), :], x_ref[place(x, 1, 1), :]),
        bare,
        begin,
    )

    def first_factor(source):
        def keep(x, parity, out, v):
            t[x, parity] = out

        sweep(kept(source), plus, keep)

    def clenshaw(source, target, weight):
        def keep(x, parity, out, v):
            target[x, parity] = (weight * res[x, parity] - target[x, parity]) + out

        first_factor(source)
        sweep(kept(t), minus, keep)

    def two_steps(i, carry):
        at = 5 + CHEB - 2 - 2 * i
        clenshaw(b0, b1, coefficient(at))
        clenshaw(b1, b0, coefficient(at - 1))
        return carry

    lax.fori_loop(0, (CHEB - 2) // 2, two_steps, 0)
    weight = coefficient(5)
    offset = coefficient(4)

    def finish(x, parity, out, v):
        w = (weight * res[x, parity] - b1[x, parity]) + 0.5 * out
        b1[x, parity] = w
        o_ref[place(x, parity, 0), :] = w

    first_factor(b0)
    sweep(kept(t), minus, finish)

    def image(x, parity, out, v):
        o_ref[place(x, parity, 1), :] = inverse_gamma * out - offset * v

    sweep(kept(b1), plus, image)


def inverse_kernel(gh_ref, gl_ref, b_ref, x_ref, o_ref):
    rows = x_ref.shape[0] // 8
    lanes = x_ref.shape[1]
    b = jnp.broadcast_to(b_ref[:, 0:1], (rows, lanes))
    u_re, ku_re, u_im, ku_im, v_re, kv_re, v_im, kv_im = (
        x_ref[rows_of(rows, i // 2 * 2 * rows + i % 2, 2), :] for i in range(8)
    )
    c00 = ku_re - (coupling * v_re - b * u_im)
    c01 = ku_im - (coupling * v_im + b * u_re)
    c10 = kv_re - (b * v_im - u_re)
    c11 = kv_im + (b * v_re + u_im)
    data = jnp.concatenate(
        [jnp.concatenate([c00, c10], 1), jnp.concatenate([c01, c11], 1)],
        0,
    )
    back = product(gh_ref[...], gl_ref[...], data)
    for f in range(2):
        for j in range(2):
            o_ref[rows_of(rows, f * 2 + j, 4), :] = back[
                j * rows : (j + 1) * rows, f * lanes : (f + 1) * lanes
            ]


def update_kernel(y_ref, p_ref, d_ref, ny_ref, np_ref):
    rows = y_ref.shape[1]
    for j in range(2):
        ny_ref[j] = y_ref[j] - d_ref[rows_of(rows, j, 4), :]
        np_ref[j] = p_ref[j] - d_ref[rows_of(rows, 2 + j, 4), :]


def swapped(value, distance):
    count = lax.axis_size("space")
    return lax.ppermute(value, "space", [(i, i ^ distance) for i in range(count)])


def shards(state_field, adjoint, target, initial_state, conductivity, reaction):
    steps, width_x, width_y, width_z = state_field.shape
    devices = lax.axis_size("tm")
    spaces = lax.axis_size("space")
    rows = width_x * width_y
    horizon = steps * devices
    assert steps == 2 and rows == devices and spaces == 4
    f32 = jnp.float32

    def shape(*dims):
        return jax.ShapeDtypeStruct(dims, f32)

    flat = (steps, rows, width_z)
    state_rows = state_field.reshape(flat)
    adjoint_rows = adjoint.reshape(flat)
    packed, material = pl.pallas_call(
        pack_kernel,
        out_shape=(
            shape(rows * 6, width_z),
            shape(2, width_x, width_y, width_z),
        ),
        in_specs=[hbm()] * 5,
        out_specs=(vmem(), vmem()),
        scratch_shapes=[pltpu.VMEM(flat, f32)] * 3 + [pltpu.SemaphoreType.DMA((5,))],
        name="pack",
    )(conductivity, reaction, state_rows, adjoint_rows, target.reshape(flat))
    table, twist = solver_table(horizon, devices)
    material_core = swapped(material, 1)
    material_far = swapped(material, 2)
    by_cell = lax.all_to_all(
        packed.reshape(rows * 3, 2, width_z), "tm", 0, 0, tiled=True
    ).reshape(packed.shape)
    material_both = swapped(material_far, 1)
    forward, inverse = (halves(jnp.asarray(each)) for each in time_tables(horizon, devices))
    hat = pl.pallas_call(
        forward_kernel,
        out_shape=shape(devices * 8, width_z),
        in_specs=[vmem()] * 4,
        out_specs=vmem(),
        compiler_params=grant,
        name="forward",
    )(*forward, initial_state.reshape(rows, width_z), by_cell)
    grid = (spaces * width_x, 2, width_y // 2, width_z)
    pairs = (spaces * width_x, width_y // 2, width_z)
    faces = pl.pallas_call(
        functools.partial(faces_kernel, devices),
        out_shape=(shape(*grid),) + (shape(*pairs),) * 3 + (shape(*grid),) * 5,
        in_specs=[vmem()] * 5,
        out_specs=(vmem(),) * 9,
        scratch_shapes=[pltpu.VMEM((spaces, 2, width_x, width_y, width_z), f32)],
        compiler_params=grant,
        name="faces",
    )(jnp.asarray(table), material, material_core, material_far, material_both)
    hat, faces = lax.optimization_barrier((hat, faces))
    everyone = ("space", "tm")
    by_item = lax.all_to_all(hat, everyone, 0, 0, tiled=True)
    solved = pl.pallas_call(
        functools.partial(solve_kernel, devices),
        out_shape=shape(rows * 8, width_z),
        in_specs=[vmem()] * 11,
        out_specs=vmem(),
        scratch_shapes=[pltpu.VMEM(grid, f32)] * 4,
        compiler_params=grant,
        name="solve",
    )(jnp.asarray(table), *faces, by_item)
    by_row = lax.all_to_all(solved, everyone, 0, 0, tiled=True)
    delta = pl.pallas_call(
        inverse_kernel,
        out_shape=shape(devices * 4, width_z),
        in_specs=[vmem()] * 4,
        out_specs=vmem(),
        compiler_params=grant,
        name="inverse",
    )(*inverse, jnp.asarray(twist_block(twist)), by_row)
    by_time = lax.all_to_all(delta, "tm", 0, 0, tiled=True)
    new_state, new_adjoint = pl.pallas_call(
        update_kernel,
        out_shape=(shape(*flat), shape(*flat)),
        in_specs=[vmem()] * 3,
        out_specs=(vmem(), vmem()),
        compiler_params=grant,
        name="update",
    )(state_rows, adjoint_rows, by_time)
    return new_state.reshape(state_field.shape), new_adjoint.reshape(adjoint.shape)


def solution(mesh):
    in_specs = (
        P("tm", "space", None, None),
        P("tm", "space", None, None),
        P("tm", "space", None, None),
        P("space", None, None),
        P("space", None, None),
        P("space", None, None),
    )
    out_specs = (P("tm", "space", None, None), P("tm", "space", None, None))
    return jax.shard_map(
        shards, mesh=mesh, in_specs=in_specs, out_specs=out_specs, check_vma=False
    )
```

profile of v0, /device:TPU:1, one launch (start us, length us, event | category | flops | bytes accessed | tf_op | source)
XLA Modules:
  0.0 90.9 jit_solution(732980752255995605)
XLA Ops:
  0.6 0.0 copy-start
  0.6 1.7 %pack.1 = (f32[384,128]{1,0:T(8,128)}, f32[2,4,16,128]{3,2,1,0:T(8,128)}) custom-call(f32[4,16,128]{2,1,0:T(8,128)} %c_hbm.1, f32[4,16,128]{2,1,0:T(8,128)} %r_hbm.1, f32[2,64,128]{2,1,0:T(8,128)} %bitcast.21, f32[2,64,128]{2,1,0:T(8,128)} %bitcast.23, f32[2,64,128]{2,1,0:T(8,128)} %bitcast.27), custom_call_target="tpu_custom_call" | custom-call | tf_op jit(solution)/shard_map/pack/pallas_call | solution.py:370
  2.4 0.0 copy-start.3
  2.4 12.7 %all-to-all-start = ((f32[192,2,128]{2,1,0:T(2,128)}), f32[192,2,128]{2,1,0:T(2,128)S(1)}, u32[]{:S(2)}, u32[]{:S(2)}) async-start(f32[192,2,128]{2,1,0:T(2,128)} %bitcast.26), calls=%async_computation | async-start | bytes 393216 | tf_op jit(solution)/shard_map/all_to_all | solution.py:384
  15.1 0.0 copy-start.4
  15.1 0.0 copy-start.5
  15.1 0.0 copy-start.6
  15.1 4.3 %collective-permute-start.1 = (f32[2,4,16,128]{3,2,1,0:T(8,128)S(1)}, f32[2,4,16,128]{3,2,1,0:T(8,128)S(1)}, u32[]{:S(2)}, u32[]{:S(2)}) collective-permute-start(f32[2,4,16,128]{3,2,1,0:T(8,128)S(1)} %copy-done.3), channel_id=1, source_target_pairs={{0,2},{1,3},{2,0},{3,1},{4,6},{5,7},{6,4},{7,5},{8,10},{9,11},{10,... | collective-permute-start | bytes 196616 | tf_op jit(solution)/shard_map/ppermute | solution.py:352
  19.4 1.2 %collective-permute-start = (f32[2,4,16,128]{3,2,1,0:T(8,128)S(1)}, f32[2,4,16,128]{3,2,1,0:T(8,128)S(1)}, u32[]{:S(2)}, u32[]{:S(2)}) collective-permute-start(f32[2,4,16,128]{3,2,1,0:T(8,128)S(1)} %copy-done.3), channel_id=1, source_target_pairs={{0,1},{1,0},{2,3},{3,2},{4,5},{5,4},{6,7},{7,6},{8,9},{9,8},{10,11... | collective-permute-start | bytes 196616 | tf_op jit(solution)/shard_map/ppermute | solution.py:352
  20.6 3.0 %collective-permute-done.1.m2_ref = f32[2,4,16,128]{3,2,1,0:T(8,128)S(1)} collective-permute-done((f32[2,4,16,128]{3,2,1,0:T(8,128)S(1)}, f32[2,4,16,128]{3,2,1,0:T(8,128)S(1)}, u32[]{:S(2)}, u32[]{:S(2)}) %collective-permute-start.1) | collective-permute-done | bytes 65568 | tf_op jit(solution)/shard_map/ppermute | solution.py:352
  23.7 1.5 %collective-permute-start.2 = (f32[2,4,16,128]{3,2,1,0:T(8,128)S(1)}, f32[2,4,16,128]{3,2,1,0:T(8,128)S(1)}, u32[]{:S(2)}, u32[]{:S(2)}) collective-permute-start(f32[2,4,16,128]{3,2,1,0:T(8,128)S(1)} %collective-permute-done.1.m2_ref), channel_id=1, source_target_pairs={{0,1},{1,0},{2,3},{3,2},{4,5},{5,4},{6,7},{7,6},{8,9},{9,8},{10,11... | collective-permute-start | bytes 196616 | tf_op jit(solution)/shard_map/ppermute | solution.py:352
  25.2 0.0 collective-permute-done.m1_ref
  25.2 0.9 collective-permute-done.2.m3_ref
  26.1 0.2 faces.1
  26.3 0.0 all-to-all-done
  26.3 0.0 copy-done.4
  26.3 0.0 copy-done.5
  26.3 0.0 copy-done.6
  26.3 0.3 forward.1
  26.6 26.6 %all_to_all.38 = f32[256,2,128]{2,1,0:T(2,128)S(1)} all-to-all(f32[256,2,128]{2,1,0:T(2,128)S(1)} %bitcast.14), channel_id=1, replica_groups=mesh['tm'=64,'space'=4] {'space','tm'}, dimensions={0} | all-to-all | bytes 524288 | tf_op jit(solution)/shard_map/all_to_all | solution.py:410
  53.2 1.7 %solve.1 = f32[512,128]{1,0:T(8,128)S(1)} custom-call(f32[1040,128]{1,0:T(8,128)S(1)} %copy-done, f32[16,2,8,128]{3,2,1,0:T(8,128)S(1)} %get-tuple-element.36.cx, f32[16,8,128]{2,1,0:T(8,128)S(1)} %get-tuple-element.37.cy, f32[16,8,128]{2,1,0:T(8,128)S(1)} %get-tuple-element.38.cy_next, f32[16,8,128]{2,1,0:T(8,128)S(1)} %get-tuple-element.39.cy_last, ...), custom_call_target="tpu_custom_call" | custom-call | tf_op jit(solution)/shard_map/solve/pallas_call | solution.py:411
  54.9 0.0 copy-start.7
  54.9 0.0 copy-start.8
  54.9 0.0 copy-start.9
  54.9 20.4 %all_to_all.39 = f32[256,2,128]{2,1,0:T(2,128)S(1)} all-to-all(f32[256,2,128]{2,1,0:T(2,128)S(1)} %bitcast.17), channel_id=1, replica_groups=mesh['tm'=64,'space'=4] {'space','tm'}, dimensions={0} | all-to-all | bytes 524288 | tf_op jit(solution)/shard_map/all_to_all | solution.py:420
  75.3 0.0 copy-done.7
  75.3 0.0 copy-done.9
  75.3 0.3 inverse.1
  75.6 0.0 copy-start.1
  75.6 0.0 copy-start.2
  75.6 14.6 %all_to_all.40 = f32[64,4,128]{2,1,0:T(4,128)S(1)} all-to-all(f32[64,4,128]{2,1,0:T(4,128)S(1)} %bitcast.20), channel_id=1, replica_groups=mesh['tm'=64,'space'=4] {'tm'}, dimensions={0} | all-to-all | bytes 262144 | tf_op jit(solution)/shard_map/all_to_all | solution.py:429
  90.2 0.7 update.1
  (5 shorter events, 0.0 us)
Async XLA Ops:
  0.6 25.5 %copy-start = (f32[1040,128]{1,0:T(8,128)S(1)}, f32[1040,128]{1,0:T(8,128)}, u32[]{:S(2)}) copy-start(f32[1040,128]{1,0:T(8,128)} %constant.10.clone.co_ref) | copy-start | bytes 1597444
  2.4 12.7 %copy-start.3 = (f32[2,4,16,128]{3,2,1,0:T(8,128)S(1)}, f32[2,4,16,128]{3,2,1,0:T(8,128)}, u32[]{:S(2)}) copy-start(f32[2,4,16,128]{3,2,1,0:T(8,128)} %get-tuple-element.26.m0_ref) | copy-start | bytes 196612
  2.4 23.9 %all-to-all-start = ((f32[192,2,128]{2,1,0:T(2,128)}), f32[192,2,128]{2,1,0:T(2,128)S(1)}, u32[]{:S(2)}, u32[]{:S(2)}) async-start(f32[192,2,128]{2,1,0:T(2,128)} %bitcast.26), calls=%async_computation | async-start | bytes 393216 | tf_op jit(solution)/shard_map/all_to_all | solution.py:384
  15.1 11.2 %copy-start.4 = (f32[4,16,128]{2,1,0:T(8,128)S(1)}, f32[4,16,128]{2,1,0:T(8,128)}, u32[]{:S(2)}) copy-start(f32[4,16,128]{2,1,0:T(8,128)} %param.13) | copy-start | bytes 98308
  15.1 11.2 %copy-start.5 = (bf16[128,128]{1,0:T(8,128)(2,1)S(1)}, bf16[128,128]{1,0:T(8,128)(2,1)}, u32[]{:S(2)}) copy-start(bf16[128,128]{1,0:T(8,128)(2,1)} %constant.22.fl_ref) | copy-start | bytes 98308
  15.1 11.2 %copy-start.6 = (bf16[128,128]{1,0:T(8,128)(2,1)S(1)}, bf16[128,128]{1,0:T(8,128)(2,1)}, u32[]{:S(2)}) copy-start(bf16[128,128]{1,0:T(8,128)(2,1)} %constant.19.fh_ref) | copy-start | bytes 98308
  15.1 8.6 %collective-permute-start.1 = (f32[2,4,16,128]{3,2,1,0:T(8,128)S(1)}, f32[2,4,16,128]{3,2,1,0:T(8,128)S(1)}, u32[]{:S(2)}, u32[]{:S(2)}) collective-permute-start(f32[2,4,16,128]{3,2,1,0:T(8,128)S(1)} %copy-done.3), channel_id=1, source_target_pairs={{0,2},{1,3},{2,0},{3,1},{4,6},{5,7},{6,4},{7,5},{8,10},{9,11},{10,... | collective-permute-start | bytes 196616 | tf_op jit(solution)/shard_map/ppermute | solution.py:352
  19.4 5.8 %collective-permute-start = (f32[2,4,16,128]{3,2,1,0:T(8,128)S(1)}, f32[2,4,16,128]{3,2,1,0:T(8,128)S(1)}, u32[]{:S(2)}, u32[]{:S(2)}) collective-permute-start(f32[2,4,16,128]{3,2,1,0:T(8,128)S(1)} %copy-done.3), channel_id=1, source_target_pairs={{0,1},{1,0},{2,3},{3,2},{4,5},{5,4},{6,7},{7,6},{8,9},{9,8},{10,11... | collective-permute-start | bytes 196616 | tf_op jit(solution)/shard_map/ppermute | solution.py:352
  23.7 2.4 %collective-permute-start.2 = (f32[2,4,16,128]{3,2,1,0:T(8,128)S(1)}, f32[2,4,16,128]{3,2,1,0:T(8,128)S(1)}, u32[]{:S(2)}, u32[]{:S(2)}) collective-permute-start(f32[2,4,16,128]{3,2,1,0:T(8,128)S(1)} %collective-permute-done.1.m2_ref), channel_id=1, source_target_pairs={{0,1},{1,0},{2,3},{3,2},{4,5},{5,4},{6,7},{7,6},{8,9},{9,8},{10,11... | collective-permute-start | bytes 196616 | tf_op jit(solution)/shard_map/ppermute | solution.py:352
  54.9 20.4 %copy-start.7 = (bf16[128,128]{1,0:T(8,128)(2,1)S(1)}, bf16[128,128]{1,0:T(8,128)(2,1)}, u32[]{:S(2)}) copy-start(bf16[128,128]{1,0:T(8,128)(2,1)} %constant.18.gl_ref) | copy-start | bytes 98308
  54.9 20.4 %copy-start.8 = (bf16[128,128]{1,0:T(8,128)(2,1)S(1)}, bf16[128,128]{1,0:T(8,128)(2,1)}, u32[]{:S(2)}) copy-start(bf16[128,128]{1,0:T(8,128)(2,1)} %constant.15.gh_ref) | copy-start | bytes 98308
  54.9 20.4 %copy-start.9 = (f32[64,128]{1,0:T(8,128)S(1)}, f32[64,128]{1,0:T(8,128)}, u32[]{:S(2)}) copy-start(f32[64,128]{1,0:T(8,128)} %constant.11.clone.b_ref) | copy-start | bytes 98308
  75.6 14.6 %copy-start.1 = (f32[2,4,16,128]{3,2,1,0:T(8,128)S(1)}, f32[2,4,16,128]{3,2,1,0:T(8,128)}, u32[]{:S(2)}) copy-start(f32[2,4,16,128]{3,2,1,0:T(8,128)} %param.10) | copy-start | bytes 196612
  75.6 14.6 %copy-start.2 = (f32[2,4,16,128]{3,2,1,0:T(8,128)S(1)}, f32[2,4,16,128]{3,2,1,0:T(8,128)}, u32[]{:S(2)}) copy-start(f32[2,4,16,128]{3,2,1,0:T(8,128)} %param.11) | copy-start | bytes 196612
where the time goes:
time: 91.3 us; the launch traced here: 90.9 us
  blocking collectives  61.6 us (67%)
  starting transfers between devices  19.7 us (22%)
  Pallas kernels  4.8 us (5%)
  waiting for transfers between devices  3.93 us (4%)
    all_to_all x1, blocking collectives, shards(): by_item = lax.all_to_all(hat, everyone, 0, 0, tiled=True)  26.6 us
    all_to_all x1, blocking collectives, shards(): by_row = lax.all_to_all(solved, everyone, 0, 0, tiled=True)  20.4 us
    all_to_all x1, blocking collectives, shards(): by_time = lax.all_to_all(delta, 'tm', 0, 0, tiled=True)  14.6 us
    all_to_all x1, starting transfers between devices, shards(): lax.all_to_all(packed.reshape(rows * 3, 2, width_z), 'tm', 0, 0, tiled=True)  12.7 us
    ppermute x3, starting transfers between devices, swapped(): lax.ppermute(value, 'space', [(i, i ^ distance) for i in range(count)])  7.07 us
    ppermute x3, waiting for transfers between devices, swapped(): lax.ppermute(value, 'space', [(i, i ^ distance) for i in range(count)])  3.92 us
  transfers between devices with their start and end apart: 4, of which 2 were waited for; matrix products, arithmetic and copies ran while one was open for 0% of the time, Pallas kernels for 0%

commit v1 on v0

--- a/solution.py
+++ b/solution.py
@@ -352,6 +352,18 @@
     return lax.ppermute(value, "space", [(i, i ^ distance) for i in range(count)])
 
 
+def mirrored(value, distance):
+    spaces = lax.axis_size("space")
+    devices = lax.axis_size("tm")
+    layers = 4
+    share = devices // layers
+    pairs = []
+    for tm in range(devices):
+        other = (layers - 1 - tm // share) * share + tm % share
+        pairs += [(tm * spaces + i, other * spaces + (i ^ distance)) for i in range(spaces)]
+    return lax.ppermute(value, ("tm", "space"), pairs)
+
+
 def shards(state_field, adjoint, target, initial_state, conductivity, reaction):
     steps, width_x, width_y, width_z = state_field.shape
     devices = lax.axis_size("tm")
@@ -376,11 +388,23 @@
         in_specs=[hbm()] * 5,
         out_specs=(vmem(), vmem()),
         scratch_shapes=[pltpu.VMEM(flat, f32)] * 3 + [pltpu.SemaphoreType.DMA((5,))],
+        compiler_params=grant,
         name="pack",
-    )(conductivity, reaction, state_rows, adjoint_rows, target.reshape(flat))
+    )(
+        *(
+            pltpu.with_memory_space_constraint(each, pltpu.HBM)
+            for each in (
+                conductivity,
+                reaction,
+                state_rows,
+                adjoint_rows,
+                target.reshape(flat),
+            )
+        )
+    )
     table, twist = solver_table(horizon, devices)
     material_core = swapped(material, 1)
-    material_far = swapped(material, 2)
+    material_far = mirrored(material, 2)
     by_cell = lax.all_to_all(
         packed.reshape(rows * 3, 2, width_z), "tm", 0, 0, tiled=True
     ).reshape(packed.shape)

time: 91.3 us -> 89.5 us (0.980)
  waiting for transfers between devices: 3.93 us -> 2.15 us
    ppermute x0 -> x1, starting transfers between devices: none -> 4.34 us  [mirrored(): return lax.ppermute(value, ('tm', 'space'), pairs)]
    ppermute x3 -> x2, starting transfers between devices: 7.07 us -> 3.51 us  [swapped(): lax.ppermute(value, 'space', [(i, i ^ distance) for i in range(count)])]
    ppermute x3 -> x2, waiting for transfers between devices: 3.92 us -> 0.9 us  [swapped(): lax.ppermute(value, 'space', [(i, i ^ distance) for i in range(count)])]
  transfers between devices with their start and end apart: 4 -> 4, of which waited for: 2 -> 3; matrix products, arithmetic and copies ran while one was open for 0% -> 0% of each run, Pallas kernels for 0% -> 0%
where the time goes in v1:
time: 89.5 us; the launch traced here: 89.1 us
  blocking collectives  61 us (68%)
  starting transfers between devices  20.4 us (23%)
  Pallas kernels  4.79 us (5%)
  waiting for transfers between devices  2.15 us (2%)
    all_to_all x1, blocking collectives, shards(): by_item = lax.all_to_all(hat, everyone, 0, 0, tiled=True)  26 us
    all_to_all x1, blocking collectives, shards(): by_row = lax.all_to_all(solved, everyone, 0, 0, tiled=True)  20.4 us
    all_to_all x1, blocking collectives, shards(): by_time = lax.all_to_all(delta, 'tm', 0, 0, tiled=True)  14.6 us
    all_to_all x1, starting transfers between devices, shards(): lax.all_to_all(packed.reshape(rows * 3, 2, width_z), 'tm', 0, 0, tiled=True)  12.6 us
    ppermute x1, starting transfers between devices, mirrored(): return lax.ppermute(value, ('tm', 'space'), pairs)  4.34 us
    ppermute x2, starting transfers between devices, swapped(): lax.ppermute(value, 'space', [(i, i ^ distance) for i in range(count)])  3.51 us
  transfers between devices with their start and end apart: 4, of which 3 were waited for; matrix products, arithmetic and copies ran while one was open for 0% of the time, Pallas kernels for 0%

profile of v1, /device:TPU:1, one launch (start us, length us, event | category | flops | bytes accessed | tf_op | source)
XLA Modules:
  0.0 89.1 jit_solution(1603547593046772408)
XLA Ops:
  0.6 0.0 copy-start
  0.6 1.7 %pack.1 = (f32[384,128]{1,0:T(8,128)}, f32[2,4,16,128]{3,2,1,0:T(8,128)S(1)}) custom-call(f32[4,16,128]{2,1,0:T(8,128)} %c_hbm.1, f32[4,16,128]{2,1,0:T(8,128)} %r_hbm.1, f32[2,64,128]{2,1,0:T(8,128)} %bitcast.21, f32[2,64,128]{2,1,0:T(8,128)} %bitcast.23, f32[2,64,128]{2,1,0:T(8,128)} %bitcast.26), custom_call_target="tpu_custom_call" | custom-call | tf_op jit(solution)/shard_map/pack/pallas_call | solution.py:382
  2.3 12.6 %all-to-all-start = ((f32[192,2,128]{2,1,0:T(2,128)}), f32[192,2,128]{2,1,0:T(2,128)S(1)}, u32[]{:S(2)}, u32[]{:S(2)}) async-start(f32[192,2,128]{2,1,0:T(2,128)} %bitcast.4), calls=%async_computation | async-start | bytes 393216 | tf_op jit(solution)/shard_map/all_to_all | solution.py:408
  14.9 0.0 copy-start.3
  14.9 0.0 copy-start.4
  14.9 0.0 copy-start.5
  14.9 4.3 %collective-permute-start.1 = (f32[2,4,16,128]{3,2,1,0:T(8,128)S(1)}, f32[2,4,16,128]{3,2,1,0:T(8,128)S(1)}, u32[]{:S(2)}, u32[]{:S(2)}) collective-permute-start(f32[2,4,16,128]{3,2,1,0:T(8,128)S(1)} %get-tuple-element.26.m0_ref), channel_id=1, source_target_pairs={{0,194},{1,195},{2,192},{3,193},{4,198},{5,199},{6,196},{7,197},{8... | collective-permute-start | bytes 196616 | tf_op jit(solution)/shard_map/ppermute | solution.py:364
  19.3 1.5 %collective-permute-start = (f32[2,4,16,128]{3,2,1,0:T(8,128)S(1)}, f32[2,4,16,128]{3,2,1,0:T(8,128)S(1)}, u32[]{:S(2)}, u32[]{:S(2)}) collective-permute-start(f32[2,4,16,128]{3,2,1,0:T(8,128)S(1)} %get-tuple-element.26.m0_ref), channel_id=1, source_target_pairs={{0,1},{1,0},{2,3},{3,2},{4,5},{5,4},{6,7},{7,6},{8,9},{9,8},{10,11... | collective-permute-start | bytes 196616 | tf_op jit(solution)/shard_map/ppermute | solution.py:352
  20.8 0.4 collective-permute-done.1.m2_ref
  21.2 2.0 %collective-permute-start.2 = (f32[2,4,16,128]{3,2,1,0:T(8,128)S(1)}, f32[2,4,16,128]{3,2,1,0:T(8,128)S(1)}, u32[]{:S(2)}, u32[]{:S(2)}) collective-permute-start(f32[2,4,16,128]{3,2,1,0:T(8,128)S(1)} %collective-permute-done.1.m2_ref), channel_id=1, source_target_pairs={{0,1},{1,0},{2,3},{3,2},{4,5},{5,4},{6,7},{7,6},{8,9},{9,8},{10,11... | collective-permute-start | bytes 196616 | tf_op jit(solution)/shard_map/ppermute | solution.py:352
  23.2 0.0 collective-permute-done.m1_ref
  23.2 0.9 %collective-permute-done.2.m3_ref = f32[2,4,16,128]{3,2,1,0:T(8,128)S(1)} collective-permute-done((f32[2,4,16,128]{3,2,1,0:T(8,128)S(1)}, f32[2,4,16,128]{3,2,1,0:T(8,128)S(1)}, u32[]{:S(2)}, u32[]{:S(2)}) %collective-permute-start.2) | collective-permute-done | bytes 65568 | tf_op jit(solution)/shard_map/ppermute | solution.py:352
  24.1 0.0 copy-done
  24.1 0.2 faces.1
  24.3 0.8 all-to-all-done
  25.1 0.0 copy-done.3
  25.1 0.0 copy-done.4
  25.1 0.0 copy-done.5
  25.1 0.3 forward.1
  25.4 26.0 %all_to_all.38 = f32[256,2,128]{2,1,0:T(2,128)S(1)} all-to-all(f32[256,2,128]{2,1,0:T(2,128)S(1)} %bitcast.14), channel_id=1, replica_groups=mesh['tm'=64,'space'=4] {'space','tm'}, dimensions={0} | all-to-all | bytes 524288 | tf_op jit(solution)/shard_map/all_to_all | solution.py:434
  51.4 1.7 %solve.1 = f32[512,128]{1,0:T(8,128)S(1)} custom-call(f32[1040,128]{1,0:T(8,128)S(1)} %copy-done, f32[16,2,8,128]{3,2,1,0:T(8,128)S(1)} %get-tuple-element.36.cx, f32[16,8,128]{2,1,0:T(8,128)S(1)} %get-tuple-element.37.cy, f32[16,8,128]{2,1,0:T(8,128)S(1)} %get-tuple-element.38.cy_next, f32[16,8,128]{2,1,0:T(8,128)S(1)} %get-tuple-element.39.cy_last, ...), custom_call_target="tpu_custom_call" | custom-call | tf_op jit(solution)/shard_map/solve/pallas_call | solution.py:435
  53.1 0.0 copy-start.6
  53.1 0.0 copy-start.7
  53.2 0.0 copy-start.8
  53.2 20.4 %all_to_all.39 = f32[256,2,128]{2,1,0:T(2,128)S(1)} all-to-all(f32[256,2,128]{2,1,0:T(2,128)S(1)} %bitcast.17), channel_id=1, replica_groups=mesh['tm'=64,'space'=4] {'space','tm'}, dimensions={0} | all-to-all | bytes 524288 | tf_op jit(solution)/shard_map/all_to_all | solution.py:444
  73.5 0.0 copy-done.6
  73.5 0.0 copy-done.8
  73.5 0.3 inverse.1
  73.8 0.0 copy-start.1
  73.8 0.0 copy-start.2
  73.9 14.6 %all_to_all.40 = f32[64,4,128]{2,1,0:T(4,128)S(1)} all-to-all(f32[64,4,128]{2,1,0:T(4,128)S(1)} %bitcast.20), channel_id=1, replica_groups=mesh['tm'=64,'space'=4] {'tm'}, dimensions={0} | all-to-all | bytes 262144 | tf_op jit(solution)/shard_map/all_to_all | solution.py:453
  88.5 0.7 update.1
  (3 shorter events, 0.0 us)
Async XLA Ops:
  0.6 23.5 %copy-start = (f32[1040,128]{1,0:T(8,128)S(1)}, f32[1040,128]{1,0:T(8,128)}, u32[]{:S(2)}) copy-start(f32[1040,128]{1,0:T(8,128)} %constant.10.clone.co_ref) | copy-start | bytes 1597444
  2.3 22.8 %all-to-all-start = ((f32[192,2,128]{2,1,0:T(2,128)}), f32[192,2,128]{2,1,0:T(2,128)S(1)}, u32[]{:S(2)}, u32[]{:S(2)}) async-start(f32[192,2,128]{2,1,0:T(2,128)} %bitcast.4), calls=%async_computation | async-start | bytes 393216 | tf_op jit(solution)/shard_map/all_to_all | solution.py:408
  14.9 10.2 %copy-start.3 = (f32[4,16,128]{2,1,0:T(8,128)S(1)}, f32[4,16,128]{2,1,0:T(8,128)}, u32[]{:S(2)}) copy-start(f32[4,16,128]{2,1,0:T(8,128)} %param.13) | copy-start | bytes 98308
  14.9 10.2 %copy-start.4 = (bf16[128,128]{1,0:T(8,128)(2,1)S(1)}, bf16[128,128]{1,0:T(8,128)(2,1)}, u32[]{:S(2)}) copy-start(bf16[128,128]{1,0:T(8,128)(2,1)} %constant.22.fl_ref) | copy-start | bytes 98308
  14.9 10.2 %copy-start.5 = (bf16[128,128]{1,0:T(8,128)(2,1)S(1)}, bf16[128,128]{1,0:T(8,128)(2,1)}, u32[]{:S(2)}) copy-start(bf16[128,128]{1,0:T(8,128)(2,1)} %constant.19.fh_ref) | copy-start | bytes 98308
  14.9 6.3 %collective-permute-start.1 = (f32[2,4,16,128]{3,2,1,0:T(8,128)S(1)}, f32[2,4,16,128]{3,2,1,0:T(8,128)S(1)}, u32[]{:S(2)}, u32[]{:S(2)}) collective-permute-start(f32[2,4,16,128]{3,2,1,0:T(8,128)S(1)} %get-tuple-element.26.m0_ref), channel_id=1, source_target_pairs={{0,194},{1,195},{2,192},{3,193},{4,198},{5,199},{6,196},{7,197},{8... | collective-permute-start | bytes 196616 | tf_op jit(solution)/shard_map/ppermute | solution.py:364
  19.3 3.9 %collective-permute-start = (f32[2,4,16,128]{3,2,1,0:T(8,128)S(1)}, f32[2,4,16,128]{3,2,1,0:T(8,128)S(1)}, u32[]{:S(2)}, u32[]{:S(2)}) collective-permute-start(f32[2,4,16,128]{3,2,1,0:T(8,128)S(1)} %get-tuple-element.26.m0_ref), channel_id=1, source_target_pairs={{0,1},{1,0},{2,3},{3,2},{4,5},{5,4},{6,7},{7,6},{8,9},{9,8},{10,11... | collective-permute-start | bytes 196616 | tf_op jit(solution)/shard_map/ppermute | solution.py:352
  21.2 2.9 %collective-permute-start.2 = (f32[2,4,16,128]{3,2,1,0:T(8,128)S(1)}, f32[2,4,16,128]{3,2,1,0:T(8,128)S(1)}, u32[]{:S(2)}, u32[]{:S(2)}) collective-permute-start(f32[2,4,16,128]{3,2,1,0:T(8,128)S(1)} %collective-permute-done.1.m2_ref), channel_id=1, source_target_pairs={{0,1},{1,0},{2,3},{3,2},{4,5},{5,4},{6,7},{7,6},{8,9},{9,8},{10,11... | collective-permute-start | bytes 196616 | tf_op jit(solution)/shard_map/ppermute | solution.py:352
  53.1 20.4 %copy-start.6 = (bf16[128,128]{1,0:T(8,128)(2,1)S(1)}, bf16[128,128]{1,0:T(8,128)(2,1)}, u32[]{:S(2)}) copy-start(bf16[128,128]{1,0:T(8,128)(2,1)} %constant.18.gl_ref) | copy-start | bytes 98308
  53.1 20.4 %copy-start.7 = (bf16[128,128]{1,0:T(8,128)(2,1)S(1)}, bf16[128,128]{1,0:T(8,128)(2,1)}, u32[]{:S(2)}) copy-start(bf16[128,128]{1,0:T(8,128)(2,1)} %constant.15.gh_ref) | copy-start | bytes 98308
  53.2 20.4 %copy-start.8 = (f32[64,128]{1,0:T(8,128)S(1)}, f32[64,128]{1,0:T(8,128)}, u32[]{:S(2)}) copy-start(f32[64,128]{1,0:T(8,128)} %constant.11.clone.b_ref) | copy-start | bytes 98308
  73.8 14.6 %copy-start.1 = (f32[2,4,16,128]{3,2,1,0:T(8,128)S(1)}, f32[2,4,16,128]{3,2,1,0:T(8,128)}, u32[]{:S(2)}) copy-start(f32[2,4,16,128]{3,2,1,0:T(8,128)} %param.10) | copy-start | bytes 196612
  73.8 14.6 %copy-start.2 = (f32[2,4,16,128]{3,2,1,0:T(8,128)S(1)}, f32[2,4,16,128]{3,2,1,0:T(8,128)}, u32[]{:S(2)}) copy-start(f32[2,4,16,128]{3,2,1,0:T(8,128)} %param.11) | copy-start | bytes 196612

commit v2 on v1

--- a/solution.py
+++ b/solution.py
@@ -81,27 +81,21 @@
     return pl.ds(start, count, stride=stride)
 
 
-def pack_kernel(c_hbm, r_hbm, y_hbm, p_hbm, t_hbm, o_ref, m_ref, y_ref, p_ref, t_ref, sem):
+def pack_kernel(c_hbm, r_hbm, y_hbm, p_hbm, t_hbm, o_hbm, m_ref, sem):
+    pairs = [
+        (each.at[j], o_hbm.at[:, 2 * i + j, 0, :])
+        for i, each in enumerate((y_hbm, p_hbm, t_hbm))
+        for j in range(2)
+    ]
+    pairs += [(c_hbm, m_ref.at[0]), (r_hbm, m_ref.at[1])]
     copies = [
         pltpu.make_async_copy(source, target, sem.at[i])
-        for i, (source, target) in enumerate(
-            (
-                (y_hbm, y_ref),
-                (p_hbm, p_ref),
-                (t_hbm, t_ref),
-                (c_hbm, m_ref.at[0]),
-                (r_hbm, m_ref.at[1]),
-            )
-        )
+        for i, (source, target) in enumerate(pairs)
     ]
     for copy in copies:
         copy.start()
     for copy in copies:
         copy.wait()
-    rows = y_ref.shape[1]
-    for i, ref in enumerate((y_ref, p_ref, t_ref)):
-        for j in range(2):
-            o_ref[rows_of(rows, 2 * i + j, 6), :] = ref[j]
 
 
 def halves(value):
@@ -382,12 +376,12 @@
     packed, material = pl.pallas_call(
         pack_kernel,
         out_shape=(
-            shape(rows * 6, width_z),
+            shape(rows, 6, 1, width_z),
             shape(2, width_x, width_y, width_z),
         ),
         in_specs=[hbm()] * 5,
-        out_specs=(vmem(), vmem()),
-        scratch_shapes=[pltpu.VMEM(flat, f32)] * 3 + [pltpu.SemaphoreType.DMA((5,))],
+        out_specs=(hbm(), vmem()),
+        scratch_shapes=[pltpu.SemaphoreType.DMA((8,))],
         compiler_params=grant,
         name="pack",
     )(
@@ -407,7 +401,7 @@
     material_far = mirrored(material, 2)
     by_cell = lax.all_to_all(
         packed.reshape(rows * 3, 2, width_z), "tm", 0, 0, tiled=True
-    ).reshape(packed.shape)
+    ).reshape(rows * 6, width_z)
     material_both = swapped(material_far, 1)
     forward, inverse = (halves(jnp.asarray(each)) for each in time_tables(horizon, devices))
     hat = pl.pallas_call(

time: 89.5 us -> 94.9 us (1.060)
  Pallas kernels: 4.79 us -> 10.2 us
    pallas_call x1, Pallas kernels: 1.7 us -> 7.13 us  [shards(): pl.pallas_call(pack_kernel, out_shape=(shape(rows, 6, 1, width_z), shape(...]
where the time goes in v2:
time: 94.9 us; the launch traced here: 94.6 us
  blocking collectives  61 us (64%)
  starting transfers between devices  20.4 us (21%)
  Pallas kernels  10.2 us (11%)
  waiting for transfers between devices  2.15 us (2%)
    all_to_all x1, blocking collectives, shards(): by_item = lax.all_to_all(hat, everyone, 0, 0, tiled=True)  26 us
    all_to_all x1, blocking collectives, shards(): by_row = lax.all_to_all(solved, everyone, 0, 0, tiled=True)  20.4 us
    all_to_all x1, blocking collectives, shards(): by_time = lax.all_to_all(delta, 'tm', 0, 0, tiled=True)  14.6 us
    all_to_all x1, starting transfers between devices, shards(): lax.all_to_all(packed.reshape(rows * 3, 2, width_z), 'tm', 0, 0, tiled=True)  12.6 us
    pallas_call x1, Pallas kernels, shards(): pl.pallas_call(pack_kernel, out_shape=(shape(rows, 6, 1, width_z), shape(...  7.13 us
    ppermute x1, starting transfers between devices, mirrored(): return lax.ppermute(value, ('tm', 'space'), pairs)  4.34 us
    ppermute x2, starting transfers between devices, swapped(): lax.ppermute(value, 'space', [(i, i ^ distance) for i in range(count)])  3.51 us
  transfers between devices with their start and end apart: 4, of which 3 were waited for; matrix products, arithmetic and copies ran while one was open for 0% of the time, Pallas kernels for 0%

profile of v2, /device:TPU:1, one launch (start us, length us, event | category | flops | bytes accessed | tf_op | source)
XLA Modules:
  0.0 94.6 jit_solution(3457788075385531429)
XLA Ops:
  0.6 0.0 copy-start
  0.6 7.1 %pack.1 = (f32[64,6,1,128]{3,2,1,0:T(1,128)}, f32[2,4,16,128]{3,2,1,0:T(8,128)S(1)}) custom-call(f32[4,16,128]{2,1,0:T(8,128)} %c_hbm.1, f32[4,16,128]{2,1,0:T(8,128)} %r_hbm.1, f32[2,64,128]{2,1,0:T(8,128)} %bitcast.21, f32[2,64,128]{2,1,0:T(8,128)} %bitcast.23, f32[2,64,128]{2,1,0:T(8,128)} %bitcast.26), custom_call_target="tpu_custom_call" | custom-call | tf_op jit(solution)/shard_map/pack/pallas_call | solution.py:376
  7.8 12.6 %all-to-all-start = ((f32[192,2,128]{2,1,0:T(2,128)}), f32[192,2,128]{2,1,0:T(2,128)S(1)}, u32[]{:S(2)}, u32[]{:S(2)}) async-start(f32[192,2,128]{2,1,0:T(2,128)} %bitcast.4), calls=%async_computation | async-start | bytes 393216 | tf_op jit(solution)/shard_map/all_to_all | solution.py:402
  20.3 0.0 copy-start.3
  20.4 0.0 copy-start.4
  20.4 0.0 copy-start.5
  20.4 4.3 %collective-permute-start.1 = (f32[2,4,16,128]{3,2,1,0:T(8,128)S(1)}, f32[2,4,16,128]{3,2,1,0:T(8,128)S(1)}, u32[]{:S(2)}, u32[]{:S(2)}) collective-permute-start(f32[2,4,16,128]{3,2,1,0:T(8,128)S(1)} %get-tuple-element.26.m0_ref), channel_id=1, source_target_pairs={{0,194},{1,195},{2,192},{3,193},{4,198},{5,199},{6,196},{7,197},{8... | collective-permute-start | bytes 196616 | tf_op jit(solution)/shard_map/ppermute | solution.py:358
  24.7 1.5 %collective-permute-start = (f32[2,4,16,128]{3,2,1,0:T(8,128)S(1)}, f32[2,4,16,128]{3,2,1,0:T(8,128)S(1)}, u32[]{:S(2)}, u32[]{:S(2)}) collective-permute-start(f32[2,4,16,128]{3,2,1,0:T(8,128)S(1)} %get-tuple-element.26.m0_ref), channel_id=1, source_target_pairs={{0,1},{1,0},{2,3},{3,2},{4,5},{5,4},{6,7},{7,6},{8,9},{9,8},{10,11... | collective-permute-start | bytes 196616 | tf_op jit(solution)/shard_map/ppermute | solution.py:346
  26.2 0.4 collective-permute-done.1.m2_ref
  26.7 2.0 %collective-permute-start.2 = (f32[2,4,16,128]{3,2,1,0:T(8,128)S(1)}, f32[2,4,16,128]{3,2,1,0:T(8,128)S(1)}, u32[]{:S(2)}, u32[]{:S(2)}) collective-permute-start(f32[2,4,16,128]{3,2,1,0:T(8,128)S(1)} %collective-permute-done.1.m2_ref), channel_id=1, source_target_pairs={{0,1},{1,0},{2,3},{3,2},{4,5},{5,4},{6,7},{7,6},{8,9},{9,8},{10,11... | collective-permute-start | bytes 196616 | tf_op jit(solution)/shard_map/ppermute | solution.py:346
  28.7 0.0 collective-permute-done.m1_ref
  28.7 0.9 collective-permute-done.2.m3_ref
  29.6 0.0 copy-done
  29.6 0.2 faces.1
  29.8 0.8 all-to-all-done
  30.6 0.0 copy-done.3
  30.6 0.0 copy-done.4
  30.6 0.0 copy-done.5
  30.6 0.3 forward.1
  30.8 26.0 %all_to_all.38 = f32[256,2,128]{2,1,0:T(2,128)S(1)} all-to-all(f32[256,2,128]{2,1,0:T(2,128)S(1)} %bitcast.14), channel_id=1, replica_groups=mesh['tm'=64,'space'=4] {'space','tm'}, dimensions={0} | all-to-all | bytes 524288 | tf_op jit(solution)/shard_map/all_to_all | solution.py:428
  56.9 1.7 %solve.1 = f32[512,128]{1,0:T(8,128)S(1)} custom-call(f32[1040,128]{1,0:T(8,128)S(1)} %copy-done, f32[16,2,8,128]{3,2,1,0:T(8,128)S(1)} %get-tuple-element.36.cx, f32[16,8,128]{2,1,0:T(8,128)S(1)} %get-tuple-element.37.cy, f32[16,8,128]{2,1,0:T(8,128)S(1)} %get-tuple-element.38.cy_next, f32[16,8,128]{2,1,0:T(8,128)S(1)} %get-tuple-element.39.cy_last, ...), custom_call_target="tpu_custom_call" | custom-call | tf_op jit(solution)/shard_map/solve/pallas_call | solution.py:429
  58.6 0.0 copy-start.6
  58.6 0.0 copy-start.7
  58.6 0.0 copy-start.8
  58.6 20.4 %all_to_all.39 = f32[256,2,128]{2,1,0:T(2,128)S(1)} all-to-all(f32[256,2,128]{2,1,0:T(2,128)S(1)} %bitcast.17), channel_id=1, replica_groups=mesh['tm'=64,'space'=4] {'space','tm'}, dimensions={0} | all-to-all | bytes 524288 | tf_op jit(solution)/shard_map/all_to_all | solution.py:438
  79.0 0.0 copy-done.6
  79.0 0.0 copy-done.7
  79.0 0.3 inverse.1
  79.3 0.0 copy-start.1
  79.3 0.0 copy-start.2
  79.3 14.6 %all_to_all.40 = f32[64,4,128]{2,1,0:T(4,128)S(1)} all-to-all(f32[64,4,128]{2,1,0:T(4,128)S(1)} %bitcast.20), channel_id=1, replica_groups=mesh['tm'=64,'space'=4] {'tm'}, dimensions={0} | all-to-all | bytes 262144 | tf_op jit(solution)/shard_map/all_to_all | solution.py:447
  93.9 0.7 update.1
  (3 shorter events, 0.0 us)
Async XLA Ops:
  0.6 28.9 %copy-start = (f32[1040,128]{1,0:T(8,128)S(1)}, f32[1040,128]{1,0:T(8,128)}, u32[]{:S(2)}) copy-start(f32[1040,128]{1,0:T(8,128)} %constant.10.clone.co_ref) | copy-start | bytes 1597444
  7.8 22.8 %all-to-all-start = ((f32[192,2,128]{2,1,0:T(2,128)}), f32[192,2,128]{2,1,0:T(2,128)S(1)}, u32[]{:S(2)}, u32[]{:S(2)}) async-start(f32[192,2,128]{2,1,0:T(2,128)} %bitcast.4), calls=%async_computation | async-start | bytes 393216 | tf_op jit(solution)/shard_map/all_to_all | solution.py:402
  20.3 10.2 %copy-start.3 = (f32[4,16,128]{2,1,0:T(8,128)S(1)}, f32[4,16,128]{2,1,0:T(8,128)}, u32[]{:S(2)}) copy-start(f32[4,16,128]{2,1,0:T(8,128)} %param.13) | copy-start | bytes 98308
  20.4 10.2 %copy-start.4 = (bf16[128,128]{1,0:T(8,128)(2,1)S(1)}, bf16[128,128]{1,0:T(8,128)(2,1)}, u32[]{:S(2)}) copy-start(bf16[128,128]{1,0:T(8,128)(2,1)} %constant.22.fl_ref) | copy-start | bytes 98308
  20.4 10.2 %copy-start.5 = (bf16[128,128]{1,0:T(8,128)(2,1)S(1)}, bf16[128,128]{1,0:T(8,128)(2,1)}, u32[]{:S(2)}) copy-start(bf16[128,128]{1,0:T(8,128)(2,1)} %constant.19.fh_ref) | copy-start | bytes 98308
  20.4 6.3 %collective-permute-start.1 = (f32[2,4,16,128]{3,2,1,0:T(8,128)S(1)}, f32[2,4,16,128]{3,2,1,0:T(8,128)S(1)}, u32[]{:S(2)}, u32[]{:S(2)}) collective-permute-start(f32[2,4,16,128]{3,2,1,0:T(8,128)S(1)} %get-tuple-element.26.m0_ref), channel_id=1, source_target_pairs={{0,194},{1,195},{2,192},{3,193},{4,198},{5,199},{6,196},{7,197},{8... | collective-permute-start | bytes 196616 | tf_op jit(solution)/shard_map/ppermute | solution.py:358
  24.7 3.9 %collective-permute-start = (f32[2,4,16,128]{3,2,1,0:T(8,128)S(1)}, f32[2,4,16,128]{3,2,1,0:T(8,128)S(1)}, u32[]{:S(2)}, u32[]{:S(2)}) collective-permute-start(f32[2,4,16,128]{3,2,1,0:T(8,128)S(1)} %get-tuple-element.26.m0_ref), channel_id=1, source_target_pairs={{0,1},{1,0},{2,3},{3,2},{4,5},{5,4},{6,7},{7,6},{8,9},{9,8},{10,11... | collective-permute-start | bytes 196616 | tf_op jit(solution)/shard_map/ppermute | solution.py:346
  26.7 2.9 %collective-permute-start.2 = (f32[2,4,16,128]{3,2,1,0:T(8,128)S(1)}, f32[2,4,16,128]{3,2,1,0:T(8,128)S(1)}, u32[]{:S(2)}, u32[]{:S(2)}) collective-permute-start(f32[2,4,16,128]{3,2,1,0:T(8,128)S(1)} %collective-permute-done.1.m2_ref), channel_id=1, source_target_pairs={{0,1},{1,0},{2,3},{3,2},{4,5},{5,4},{6,7},{7,6},{8,9},{9,8},{10,11... | collective-permute-start | bytes 196616 | tf_op jit(solution)/shard_map/ppermute | solution.py:346
  58.6 20.4 %copy-start.6 = (bf16[128,128]{1,0:T(8,128)(2,1)S(1)}, bf16[128,128]{1,0:T(8,128)(2,1)}, u32[]{:S(2)}) copy-start(bf16[128,128]{1,0:T(8,128)(2,1)} %constant.18.gl_ref) | copy-start | bytes 98308
  58.6 20.4 %copy-start.7 = (bf16[128,128]{1,0:T(8,128)(2,1)S(1)}, bf16[128,128]{1,0:T(8,128)(2,1)}, u32[]{:S(2)}) copy-start(bf16[128,128]{1,0:T(8,128)(2,1)} %constant.15.gh_ref) | copy-start | bytes 98308
  58.6 20.4 %copy-start.8 = (f32[64,128]{1,0:T(8,128)S(1)}, f32[64,128]{1,0:T(8,128)}, u32[]{:S(2)}) copy-start(f32[64,128]{1,0:T(8,128)} %constant.11.clone.b_ref) | copy-start | bytes 98308
  79.3 14.6 %copy-start.1 = (f32[2,4,16,128]{3,2,1,0:T(8,128)S(1)}, f32[2,4,16,128]{3,2,1,0:T(8,128)}, u32[]{:S(2)}) copy-start(f32[2,4,16,128]{3,2,1,0:T(8,128)} %param.10) | copy-start | bytes 196612
  79.3 14.6 %copy-start.2 = (f32[2,4,16,128]{3,2,1,0:T(8,128)S(1)}, f32[2,4,16,128]{3,2,1,0:T(8,128)}, u32[]{:S(2)}) copy-start(f32[2,4,16,128]{3,2,1,0:T(8,128)} %param.11) | copy-start | bytes 196612
